TPU v7x, 256 devices: a whole 4x4x8 slice. The times are simulated.
256 devices in a mesh: ctx: 8 (over x_hi, y), ep: 32 (over z, x_lo, core).
Axes of the slice: x: 4 (x_hi: 2, x_lo: 2; x = x_hi * 2 + x_lo), y: 4, z: 8, core: 2. Of those that a mesh axis runs over, the one named last changes fastest.
Arguments:
- queries: bfloat16 [32, 1024, 2048], P('ep', 'ctx'), may hold values from -28 to 28
- keys: bfloat16 [32, 1024, 256], P('ep', 'ctx'), may hold values from -6 to 6
- values: bfloat16 [32, 1024, 256], P('ep', 'ctx'), may hold values from -6 to 6
- docs: int32 [32, 1024], P('ep', 'ctx'), may hold values from 0 to 2, as said below
- resid: bfloat16 [32, 1024, 2048], P('ep', 'ctx'), may hold values from -6 to 6
- norm_gain: float32 [2048], replicated, may hold values from 0.25 to 1.75
- routes: int32 [32, 1024, 4], P('ep', 'ctx'), may hold values from 0 to 31, all different within a row; in each aligned block of 128 rows (0 to 127, 128 to 255, ..., all dimensions but the last counted through in order) at most 20 rows name the same one
- gates: float32 [32, 1024, 4], P('ep', 'ctx'), may hold values from 0.1 to 1
- w_gate: bfloat16 [32, 2048, 384], P('ep', 'ctx'), may hold values from -0.125 to 0.125
- w_up: bfloat16 [32, 2048, 384], P('ep', 'ctx'), may hold values from -0.125 to 0.125
- w_down: bfloat16 [32, 2048, 384], P('ep', 'ctx'), may hold values from -0.3125 to 0.3125
- grad_out: bfloat16 [32, 1024, 2048], P('ep', 'ctx'), may hold values from -6 to 6
Outputs:
- block_out: bfloat16 [32, 1024, 2048], P('ep', 'ctx')
- query_grad: bfloat16 [32, 1024, 2048], P('ep', 'ctx')
- key_grad: bfloat16 [32, 1024, 256], P('ep', 'ctx')
- value_grad: bfloat16 [32, 1024, 256], P('ep', 'ctx')
- resid_grad: bfloat16 [32, 1024, 2048], P('ep', 'ctx')
- gate_grad: float32 [32, 1024, 4], P('ep', 'ctx')
- w_gate_grad: bfloat16 [32, 2048, 384], P('ep', 'ctx')
- w_up_grad: bfloat16 [32, 2048, 384], P('ep', 'ctx')
- w_down_grad: bfloat16 [32, 2048, 384], P('ep', 'ctx')
Inputs may be any that keep to these rules, and one draw needn't show every extreme that they name: `docs`: each sequence holds exactly three documents, ids 0, 1 and 2, each a run of one or more positions, in this order. `routes`: the 4 entries of a token name different experts. Among the tokens of one device (the aligned blocks of 128 positions of a sequence), no expert is named more than 20 times, a bound that some block reaches.
All inputs are finite; a program needn't handle non-finite values.
Results may differ from a plain program's by a relative error of at most 0.04.
Values may be sent and summed in bfloat16 or wider, within the bound.
A program may use at most 128 MiB of HBM per device.

v0:
```python
import jax
import jax.numpy as jnp
from jax import lax
from jax.sharding import PartitionSpec as P

HD = 128


def attention_probs(query_rows, key_rows, query_docs, key_docs, query_start):
    count = query_rows.shape[0]
    total = key_rows.shape[0]
    heads_kv = key_rows.shape[1] // HD
    grouped = query_rows.reshape(count, heads_kv, -1, HD)
    keyed = key_rows.reshape(total, heads_kv, HD)
    query_places = query_start + jnp.arange(count)
    key_places = jnp.arange(total)
    allowed = (query_docs[:, None] == key_docs[None, :]) & (
        key_places[None, :] <= query_places[:, None]
    )
    offset = jnp.where(allowed, 0.0, -1e30).astype(jnp.float32)
    scores = (
        jnp.einsum("ikgd,jkd->kgij", grouped, keyed, preferred_element_type=jnp.float32)
        * float(HD) ** (-0.5)
        + offset
    )
    highest = jnp.max(scores, axis=-1, keepdims=True)
    raised = jnp.exp(scores - highest)
    return raised / jnp.sum(raised, axis=-1, keepdims=True)


def route_rows(rows, n_ep):
    return lax.all_to_all(
        rows.reshape(n_ep, -1, rows.shape[-1]), "ep", split_axis=0, concat_axis=0, tiled=True
    )


def per_device(
    queries, keys, values, docs, resid, norm_gain, routes, gates, w_gate, w_up, w_down, grad_out
):
    tok_rows = queries.shape[1]
    width = resid.shape[2]
    n_ep = lax.axis_size("ep")
    exp_dev = w_gate.shape[0]
    hidden_units = w_gate.shape[2]
    top_count = routes.shape[2]
    experts_all = exp_dev * n_ep
    capacity = max(2, (5 * tok_rows * top_count + 4 * experts_all - 1) // (4 * experts_all))
    query_start = lax.axis_index("ctx") * tok_rows
    score_scale = float(HD) ** (-0.5)
    query_rows = queries[0]
    query_docs = docs[0]
    all_keys, all_values, all_docs = (
        lax.all_gather(keys[0], "ctx", axis=0, tiled=True),
        lax.all_gather(values[0], "ctx", axis=0, tiled=True),
        lax.all_gather(docs[0], "ctx", axis=0, tiled=True),
    )
    total = all_keys.shape[0]
    heads_kv = all_keys.shape[1] // HD
    probs = attention_probs(query_rows, all_keys, query_docs, all_docs, query_start)
    probs_b = probs.astype(jnp.bfloat16)
    value_heads = all_values.reshape(total, heads_kv, HD)
    attn = jnp.einsum("kgij,jkd->ikgd", probs_b, value_heads, preferred_element_type=jnp.float32)
    attn = attn.reshape(tok_rows, width).astype(jnp.bfloat16)
    hidden_f = (
        (resid[0].astype(jnp.float32) + attn.astype(jnp.float32))
        .astype(jnp.bfloat16)
        .astype(jnp.float32)
    )
    rstd = lax.rsqrt(jnp.mean(hidden_f * hidden_f, axis=-1, keepdims=True) + 1e-06)
    normed = (hidden_f * rstd * norm_gain).astype(jnp.bfloat16)
    flat_routes = routes[0].reshape(tok_rows * top_count)
    onehot = (flat_routes[:, None] == jnp.arange(experts_all, dtype=jnp.int32)[None, :]).astype(
        jnp.int32
    )
    ranks = jnp.cumsum(onehot, axis=0) - onehot
    slots = jnp.sum(ranks * onehot, axis=-1)
    targets = flat_routes * capacity + slots
    repeated = jnp.repeat(normed, top_count, axis=0)
    outgoing = jnp.zeros((experts_all * capacity, width), jnp.bfloat16).at[targets].set(repeated)
    upstream = grad_out[0]
    upstream_rep = jnp.repeat(upstream, top_count, axis=0).astype(jnp.float32)
    gate_flat = gates[0].reshape(tok_rows * top_count)
    d_out_rows = (gate_flat[:, None] * upstream_rep).astype(jnp.bfloat16)
    outgoing_grad = (
        jnp.zeros((experts_all * capacity, width), jnp.bfloat16).at[targets].set(d_out_rows)
    )
    received = route_rows(outgoing, n_ep).reshape(n_ep, exp_dev, capacity, width)
    gate_full, up_full, down_full = (
        lax.all_gather(w_gate, "ctx", axis=1, tiled=True),
        lax.all_gather(w_up, "ctx", axis=1, tiled=True),
        lax.all_gather(w_down, "ctx", axis=1, tiled=True),
    )
    pre_gate = jnp.einsum("slcd,ldf->slcf", received, gate_full, preferred_element_type=jnp.float32)
    pre_up = jnp.einsum("slcd,ldf->slcf", received, up_full, preferred_element_type=jnp.float32)
    sigma = jax.nn.sigmoid(pre_gate)
    silu_val = pre_gate * sigma
    activ = (silu_val * pre_up).astype(jnp.bfloat16)
    expert_out = jnp.einsum(
        "slcf,ldf->slcd", activ, down_full, preferred_element_type=jnp.float32
    ).astype(jnp.bfloat16)
    returned = route_rows(expert_out, n_ep).reshape(experts_all * capacity, width)
    d_out = route_rows(outgoing_grad, n_ep).reshape(n_ep, exp_dev, capacity, width)
    d_activ = jnp.einsum("slcd,ldf->slcf", d_out, down_full, preferred_element_type=jnp.float32)
    d_gate = (d_activ * pre_up * sigma * (1.0 + pre_gate * (1.0 - sigma))).astype(jnp.bfloat16)
    d_up = (d_activ * silu_val).astype(jnp.bfloat16)
    d_row = (
        jnp.einsum("slcf,ldf->slcd", d_gate, gate_full, preferred_element_type=jnp.float32)
        + jnp.einsum("slcf,ldf->slcd", d_up, up_full, preferred_element_type=jnp.float32)
    ).astype(jnp.bfloat16)
    shard_rows = w_gate.shape[1]
    gate_term = jnp.einsum("slcd,slcf->dlf", received, d_gate, preferred_element_type=jnp.float32)
    up_term = jnp.einsum("slcd,slcf->dlf", received, d_up, preferred_element_type=jnp.float32)
    down_term = jnp.einsum("slcd,slcf->dlf", d_out, activ, preferred_element_type=jnp.float32)
    summed = lax.psum_scatter(
        jnp.stack([gate_term, up_term, down_term], axis=1)
        .reshape(shard_rows * lax.axis_size("ctx"), 3 * exp_dev * hidden_units)
        .astype(jnp.bfloat16),
        "ctx",
        scatter_dimension=0,
        tiled=True,
    ).astype(jnp.float32)
    summed = (
        summed.reshape(shard_rows, 3, exp_dev, hidden_units)
        .transpose(1, 2, 0, 3)
        .astype(jnp.bfloat16)
    )
    back_rows = route_rows(d_row, n_ep).reshape(experts_all * capacity, width)
    own_out = returned[targets].astype(jnp.float32)
    moe_sum = jnp.sum((gate_flat[:, None] * own_out).reshape(tok_rows, top_count, width), axis=1)
    block_out = (hidden_f + moe_sum).astype(jnp.bfloat16)
    gate_grad = jnp.sum(upstream_rep * own_out, axis=-1).reshape(tok_rows, top_count)
    d_normed = jnp.sum(
        back_rows[targets].astype(jnp.float32).reshape(tok_rows, top_count, width), axis=1
    )
    scaled = norm_gain * d_normed
    resid_grad = (
        upstream.astype(jnp.float32)
        + rstd * scaled
        - hidden_f * rstd**3 * jnp.mean(scaled * hidden_f, axis=-1, keepdims=True)
    )
    resid_grad = resid_grad.astype(jnp.bfloat16)
    grad_heads = resid_grad.reshape(tok_rows, heads_kv, -1, HD)
    attn_heads = attn.reshape(tok_rows, heads_kv, -1, HD)
    delta = jnp.einsum("ikgd,ikgd->kgi", grad_heads, attn_heads, preferred_element_type=jnp.float32)
    d_probs = jnp.einsum(
        "ikgd,jkd->kgij", grad_heads, value_heads, preferred_element_type=jnp.float32
    )
    d_scores = (probs * (d_probs - delta[..., None])).astype(jnp.bfloat16)
    key_heads = all_keys.reshape(total, heads_kv, HD)
    query_heads = query_rows.reshape(tok_rows, heads_kv, -1, HD)
    query_grad = (
        jnp.einsum("kgij,jkd->ikgd", d_scores, key_heads, preferred_element_type=jnp.float32)
        * score_scale
    )
    query_grad = query_grad.reshape(tok_rows, width).astype(jnp.bfloat16)
    key_terms = (
        jnp.einsum("kgij,ikgd->jkd", d_scores, query_heads, preferred_element_type=jnp.float32)
        * score_scale
    )
    value_terms = jnp.einsum(
        "kgij,ikgd->jkd", probs_b, grad_heads, preferred_element_type=jnp.float32
    )
    kv_terms = jnp.concatenate(
        [key_terms.reshape(total, heads_kv * HD), value_terms.reshape(total, heads_kv * HD)], axis=1
    )
    kv_grads = lax.psum_scatter(
        kv_terms.astype(jnp.bfloat16), "ctx", scatter_dimension=0, tiled=True
    ).astype(jnp.float32)
    key_grad = kv_grads[:, : heads_kv * HD].astype(jnp.bfloat16)
    value_grad = kv_grads[:, heads_kv * HD :].astype(jnp.bfloat16)
    return (
        block_out[None],
        query_grad[None],
        key_grad[None],
        value_grad[None],
        resid_grad[None],
        gate_grad[None],
        summed[0],
        summed[1],
        summed[2],
    )


def solution(mesh):
    return jax.shard_map(
        per_device,
        mesh=mesh,
        in_specs=(
            P("ep", "ctx", None),
            P("ep", "ctx", None),
            P("ep", "ctx", None),
            P("ep", "ctx"),
            P("ep", "ctx", None),
            P(),
            P("ep", "ctx", None),
            P("ep", "ctx", None),
            P("ep", "ctx", None),
            P("ep", "ctx", None),
            P("ep", "ctx", None),
            P("ep", "ctx", None),
        ),
        out_specs=(
            P("ep", "ctx", None),
            P("ep", "ctx", None),
            P("ep", "ctx", None),
            P("ep", "ctx", None),
            P("ep", "ctx", None),
            P("ep", "ctx", None),
            P("ep", "ctx", None),
            P("ep", "ctx", None),
            P("ep", "ctx", None),
        ),
        check_vma=False,
    )
```

profile of v0, /device:TPU:32, one launch (start us, length us, event | category | flops | bytes accessed | tf_op | source)
XLA Modules:
  0.0 645.9 jit_solution(3165984337473850861)
XLA Ops:
  9.8 31.3 %all-gather = bf16[1,1024,256]{1,2,0:T(8,128)(2,1)S(1)} all-gather(bf16[1,128,256]{1,2,0:T(8,128)(2,1)S(1)} %copy.75), channel_id=2, replica_groups=mesh['ctx'=8,'ep'=32] {'ctx'}, dimensions={1}, use_global_device_ids=true | all-gather | bytes 589824 | tf_op jit(solution)/shard_map/all_gather | solution.py:53
  42.6 22.0 %all-gather.1 = s32[1,1024]{1,0:T(1,128)S(1)} all-gather(s32[1,128]{1,0:T(1,128)} %param.15), channel_id=3, replica_groups=mesh['ctx'=8,'ep'=32] {'ctx'}, dimensions={1}, use_global_device_ids=true | all-gather | bytes 4608 | tf_op jit(solution)/shard_map/all_gather | solution.py:55
  64.7 35.0 %all-gather.2 = bf16[1,1024,256]{2,1,0:T(8,128)(2,1)S(1)} all-gather(bf16[1,128,256]{2,1,0:T(8,128)(2,1)} %param.14), channel_id=4, replica_groups=mesh['ctx'=8,'ep'=32] {'ctx'}, dimensions={1}, use_global_device_ids=true | all-gather | bytes 589824 | tf_op jit(solution)/shard_map/all_gather | solution.py:54
  100.2 4.9 fusion.69
  105.0 4.4 fusion.6
  109.5 2.0 bitcast_convert_fusion.3
  114.2 2.1 reshape.431
  118.1 5.4 scatter_custom_fusion
  123.5 2.4 reshape.391
  125.9 8.9 %all-to-all-start = ((bf16[32,20,2048]{2,1,0:T(8,128)(2,1)}), bf16[32,20,2048]{2,1,0:T(8,128)(2,1)}, u32[]{:S(2)}, u32[]{:S(2)}) async-start(bf16[32,20,2048]{2,1,0:T(8,128)(2,1)} %reshape.391), calls=%async_computation | async-start | bytes 6291456 | tf_op jit(solution)/shard_map/all_to_all | solution.py:32
  136.5 3.2 broadcast_in_dim.19
  139.7 5.3 convert_element_type.232
  145.2 6.1 scatter_custom_fusion.1
  151.3 2.3 reshape.397
  153.7 54.3 %all-to-all-done = bf16[32,20,2048]{2,1,0:T(8,128)(2,1)} async-done(((bf16[32,20,2048]{2,1,0:T(8,128)(2,1)}), bf16[32,20,2048]{2,1,0:T(8,128)(2,1)}, u32[]{:S(2)}, u32[]{:S(2)}) %all-to-all-start) | async-done | bytes 2621472 | tf_op jit(solution)/shard_map/all_to_all | solution.py:32
  207.9 4.6 all-to-all-start.2
  213.3 5.2 fusion.21
  218.5 58.1 %all-gather.7.cloned.1.call-done = bf16[1,2048,384]{2,1,0:T(8,128)(2,1)} async-done(((bf16[1,256,384]{2,1,0:T(8,128)(2,1)}), bf16[1,2048,384]{2,1,0:T(8,128)(2,1)}) %all-gather.7.cloned.1.call-update) | async-done | bytes 1572880 | tf_op jit(solution)/shard_map/all_gather | solution.py:89
  276.5 5.2 fusion.25
  281.7 49.6 %all-gather.11.cloned.1.call-done = bf16[1,2048,384]{2,1,0:T(8,128)(2,1)} async-done(((bf16[1,256,384]{2,1,0:T(8,128)(2,1)}), bf16[1,2048,384]{2,1,0:T(8,128)(2,1)}) %all-gather.11.cloned.1.call-update) | async-done | bytes 1572880 | tf_op jit(solution)/shard_map/all_gather | solution.py:91
  331.3 4.3 fusion.17
  335.6 2.8 fusion.60
  338.4 1.5 fusion.23
  341.5 3.2 copy.93
  344.7 7.8 %all-to-all-start.3 = ((bf16[32,20,2048]{2,1,0:T(8,128)(2,1)}), bf16[32,20,2048]{2,1,0:T(8,128)(2,1)}, u32[]{:S(2)}, u32[]{:S(2)}) async-start(bf16[32,20,2048]{2,1,0:T(8,128)(2,1)} %copy.93), calls=%async_computation.3 | async-start | bytes 6291456 | tf_op jit(solution)/shard_map/all_to_all | solution.py:32
  355.1 5.3 fusion.8
  360.4 65.1 %all-to-all-done.3 = bf16[32,20,2048]{2,1,0:T(8,128)(2,1)} async-done(((bf16[32,20,2048]{2,1,0:T(8,128)(2,1)}), bf16[32,20,2048]{2,1,0:T(8,128)(2,1)}, u32[]{:S(2)}, u32[]{:S(2)}) %all-to-all-start.3) | async-done | bytes 2621472 | tf_op jit(solution)/shard_map/all_to_all | solution.py:32
  425.6 3.6 reshape.400
  429.2 3.3 gather_fusion.1
  432.5 4.7 reshape.409
  437.3 4.9 reduce_sum.77
  444.1 2.7 fusion.44
  448.6 4.9 fusion.2
  453.5 2.1 copy-done.3
  458.7 4.1 fusion.9
  462.8 4.2 fusion.10
  467.0 2.5 pad_maximum_fusion
  470.8 1.6 convolution_convert_fusion
  472.4 3.1 copy.89
  475.5 5.1 all-to-all-start.1
  482.1 2.9 fusion.33
  486.0 67.5 %all-to-all-done.1 = bf16[32,20,2048]{2,1,0:T(8,128)(2,1)} async-done(((bf16[32,20,2048]{2,1,0:T(8,128)(2,1)}), bf16[32,20,2048]{2,1,0:T(8,128)(2,1)}, u32[]{:S(2)}, u32[]{:S(2)}) %all-to-all-start.1) | async-done | bytes 2621472 | tf_op jit(solution)/shard_map/all_to_all | solution.py:32
  553.5 3.8 reshape.396
  557.3 3.4 gather_fusion
  560.7 4.9 reshape.406
  565.6 2.7 multiply_reduce_fusion
  569.1 5.5 multiply_reduce_fusion.1
  577.6 57.7 %reduce-scatter.5.cloned.1.call-done = bf16[256,1152]{0,1:T(8,128)(2,1)} async-done(((bf16[2048,1152]{0,1:T(8,128)(2,1)}), bf16[256,1152]{0,1:T(8,128)(2,1)}) %reduce-scatter.5.cloned.1.call-update) | async-done | bytes 589840 | tf_op jit(solution)/shard_map/reduce_scatter | solution.py:114
  (127 shorter events, 33.6 us)
Async XLA Ops:
  7.2 92.8 %copy-start.31 = (s32[1,128]{1,0:T(1,128)S(1)}, s32[1,128]{1,0:T(1,128)}, u32[]{:S(2)}) copy-start(s32[1,128]{1,0:T(1,128)} %param.15) | copy-start | bytes 1540
  41.1 63.9 %copy-start.16 = (bf16[1,1024,256]{1,2,0:T(8,128)(2,1)}, bf16[1,1024,256]{1,2,0:T(8,128)(2,1)S(1)}, u32[]{:S(2)}) copy-start(bf16[1,1024,256]{1,2,0:T(8,128)(2,1)S(1)} %all-gather) | copy-start | bytes 1572868
  42.6 62.4 %copy-start.18 = (bf16[1,128,2048]{1,2,0:T(8,128)(2,1)}, bf16[1,128,2048]{1,2,0:T(8,128)(2,1)S(1)}, u32[]{:S(2)}) copy-start(bf16[1,128,2048]{1,2,0:T(8,128)(2,1)S(1)} %copy.142) | copy-start | bytes 1572868
  99.9 9.5 %copy-start.20 = (bf16[1,1024,256]{1,2,0:T(8,128)(2,1)}, bf16[1,1024,256]{1,2,0:T(8,128)(2,1)S(1)}, u32[]{:S(2)}) copy-start(bf16[1,1024,256]{1,2,0:T(8,128)(2,1)S(1)} %copy.78) | copy-start | bytes 1572868
  109.4 2.1 copy-start
  109.4 2.5 copy-start.9
  111.6 2.6 copy-start.6
  111.6 1.4 copy-start.29
  112.2 0.8 copy-start.12
  125.9 10.4 %copy-start.8 = (bf16[1,128,2048]{2,1,0:T(8,128)(2,1)S(1)}, bf16[1,128,2048]{2,1,0:T(8,128)(2,1)}, u32[]{:S(2)}) copy-start(bf16[1,128,2048]{2,1,0:T(8,128)(2,1)} %param.23) | copy-start | bytes 1572868
  125.9 82.0 %all-to-all-start = ((bf16[32,20,2048]{2,1,0:T(8,128)(2,1)}), bf16[32,20,2048]{2,1,0:T(8,128)(2,1)}, u32[]{:S(2)}, u32[]{:S(2)}) async-start(bf16[32,20,2048]{2,1,0:T(8,128)(2,1)} %reshape.391), calls=%async_computation | async-start | bytes 6291456 | tf_op jit(solution)/shard_map/all_to_all | solution.py:32
  134.9 78.4 %all-gather.9.cloned.1.call-start = ((), (), s32[]{:S(2)}) async-start(), calls=%async_computation.7 | async-start | bytes 1769472 | tf_op jit(solution)/shard_map/all_gather | solution.py:90
  135.6 140.9 %all-gather.7.cloned.1.call-start = ((), (), s32[]{:S(2)}) async-start(), calls=%async_computation.6 | async-start | bytes 1769472 | tf_op jit(solution)/shard_map/all_gather | solution.py:89
  139.7 5.3 copy-start.30
  207.9 123.4 %all-to-all-start.2 = ((bf16[32,20,2048]{2,1,0:T(8,128)(2,1)}), bf16[32,20,2048]{2,1,0:T(8,128)(2,1)}, u32[]{:S(2)}, u32[]{:S(2)}) async-start(bf16[32,20,2048]{2,1,0:T(8,128)(2,1)} %reshape.397), calls=%async_computation.2 | async-start | bytes 6291456 | tf_op jit(solution)/shard_map/all_to_all | solution.py:32
  212.5 118.8 %all-gather.11.cloned.1.call-start = ((), (), s32[]{:S(2)}) async-start(), calls=%async_computation.8 | async-start | bytes 1769472 | tf_op jit(solution)/shard_map/all_gather | solution.py:91
  331.3 4.3 copy-start.27
  335.6 2.8 copy-start.26
  338.4 1.6 copy-start.22
  338.4 1.6 copy-start.24
  344.7 9.2 %copy-start.10 = (bf16[1,128,2048]{2,1,0:T(8,128)(2,1)S(1)}, bf16[1,128,2048]{2,1,0:T(8,128)(2,1)}, u32[]{:S(2)}) copy-start(bf16[1,128,2048]{2,1,0:T(8,128)(2,1)} %param.16) | copy-start | bytes 1572868
  344.7 80.9 %all-to-all-start.3 = ((bf16[32,20,2048]{2,1,0:T(8,128)(2,1)}), bf16[32,20,2048]{2,1,0:T(8,128)(2,1)}, u32[]{:S(2)}, u32[]{:S(2)}) async-start(bf16[32,20,2048]{2,1,0:T(8,128)(2,1)} %copy.93), calls=%async_computation.3 | async-start | bytes 6291456 | tf_op jit(solution)/shard_map/all_to_all | solution.py:32
  352.6 223.5 %reduce-scatter.3.cloned.1.call-start = ((), (), s32[]{:S(2)}) async-start(), calls=%async_computation.9 | async-start | bytes 1179648 | tf_op jit(solution)/shard_map/reduce_scatter | solution.py:166
  437.2 6.2 copy-start.13
  442.1 4.7 copy-start.4
  442.2 2.0 copy-start.14
  443.5 3.3 copy-start.1
  446.8 1.7 copy-start.21
  448.6 7.0 %copy-start.19 = (bf16[1,128,2048]{1,2,0:T(8,128)(2,1)S(1)}, bf16[1,128,2048]{1,2,0:T(8,128)(2,1)}, u32[]{:S(2)}) copy-start(bf16[1,128,2048]{1,2,0:T(8,128)(2,1)} %copy-done.18) | copy-start | bytes 1572868
  453.5 2.1 copy-start.3
  457.1 1.6 copy-start.23
  458.4 4.4 copy-start.28
  458.4 176.9 %reduce-scatter.5.cloned.1.call-start = ((), (), s32[]{:S(2)}) async-start(), calls=%async_computation.10 | async-start | bytes 5308416 | tf_op jit(solution)/shard_map/reduce_scatter | solution.py:114
  462.8 4.2 copy-start.25
  469.4 1.4 copy-start.32
  475.5 5.2 copy-start.7
  475.5 6.5 %copy-start.17 = (bf16[1,1024,256]{1,2,0:T(8,128)(2,1)S(1)}, bf16[1,1024,256]{1,2,0:T(8,128)(2,1)}, u32[]{:S(2)}) copy-start(bf16[1,1024,256]{1,2,0:T(8,128)(2,1)} %copy-done.16) | copy-start | bytes 1572868
  475.5 77.9 %all-to-all-start.1 = ((bf16[32,20,2048]{2,1,0:T(8,128)(2,1)}), bf16[32,20,2048]{2,1,0:T(8,128)(2,1)}, u32[]{:S(2)}, u32[]{:S(2)}) async-start(bf16[32,20,2048]{2,1,0:T(8,128)(2,1)} %copy.89), calls=%async_computation.1 | async-start | bytes 6291456 | tf_op jit(solution)/shard_map/all_to_all | solution.py:32
  560.7 4.9 copy-start.2
  568.3 6.3 copy-start.5
  568.3 6.3 copy-start.11
  568.3 6.3 copy-start.15
Sparse Core Ops, SparseCore 0:
  138.3 65.5 all-gather.8
  206.5 69.9 all-gather.6
  279.1 52.1 all-gather.10
  458.5 77.0 reduce-scatter.2
  539.7 95.5 reduce-scatter.4
where the time goes:
time: 655 us; the launch traced here: 646 us
  waiting for transfers between devices  354 us (54%)
  blocking collectives  88.4 us (13%)
  local copies, waits for them, and re-layouts  73.9 us (11%)
  matrix products  50.5 us (8%)
  other arithmetic  37 us (6%)
  starting transfers between devices  27.6 us (4%)
  between operations  14.8 us (2%)
    all_to_all x4, waiting for transfers between devices, route_rows(): lax.all_to_all(rows.reshape(n_ep, -1, rows.shape[-1]), 'ep', split_axis=0...  187 us
    all_gather x1, waiting for transfers between devices, per_device(): lax.all_gather(w_gate, 'ctx', axis=1, tiled=True)  58.1 us
    reduce_scatter x1, waiting for transfers between devices, per_device(): lax.psum_scatter(jnp.stack([gate_term, up_term, down_term], axis=1).resha...  57.7 us
    all_gather x1, waiting for transfers between devices, per_device(): lax.all_gather(w_down, 'ctx', axis=1, tiled=True)  49.6 us
    all_gather x1, blocking collectives, per_device(): lax.all_gather(values[0], 'ctx', axis=0, tiled=True)  35 us
    all_gather x1, blocking collectives, per_device(): lax.all_gather(keys[0], 'ctx', axis=0, tiled=True)  31.3 us
    all_to_all x4, starting transfers between devices, route_rows(): lax.all_to_all(rows.reshape(n_ep, -1, rows.shape[-1]), 'ep', split_axis=0...  26.4 us
    all_gather x1, blocking collectives, per_device(): lax.all_gather(docs[0], 'ctx', axis=0, tiled=True)  22 us
  transfers between devices with their start and end apart: 9, of which 6 were waited for; matrix products, arithmetic and copies ran while one was open for 12% of the time, Pallas kernels for 0%

commit v1 on v0

--- a/solution.py
+++ b/solution.py
@@ -86,7 +86,15 @@
     )
     received = route_rows(outgoing, n_ep).reshape(n_ep, exp_dev, capacity, width)
     gate_full, up_full, down_full = (
-        lax.all_gather(w_gate, "ctx", axis=1, tiled=True),
+        jnp.concatenate(
+            jax.lax.all_to_all(
+                jnp.stack([w_gate] * jax.lax.psum(1, axis_name="ctx"), axis=0),
+                axis_name="ctx",
+                split_axis=0,
+                concat_axis=0,
+            ),
+            axis=1,
+        ),
         lax.all_gather(w_up, "ctx", axis=1, tiled=True),
         lax.all_gather(w_down, "ctx", axis=1, tiled=True),
     )

time: 655 us -> 624 us (0.953)
  waiting for transfers between devices: 354 us -> 307 us
  blocking collectives: 88.4 us -> 100 us
    all_gather x1 -> x0, waiting for transfers between devices: 58.1 us -> none  [per_device(): lax.all_gather(w_gate, 'ctx', axis=1, tiled=True)]
    all_gather x1, blocking collectives: 31.3 us -> 46.4 us  [per_device(): lax.all_gather(keys[0], 'ctx', axis=0, tiled=True)]
    all_gather x1, waiting for transfers between devices: 49.6 us -> 58.3 us  [per_device(): lax.all_gather(w_down, 'ctx', axis=1, tiled=True)]
    all_to_all x0 -> x1, starting transfers between devices: none -> 7.06 us  [per_device(): jax.lax.all_to_all(jnp.stack([w_gate] * jax.lax.psum(1, axis_name='ctx'),...]
  transfers between devices with their start and end apart: 9 -> 9, of which waited for: 6 -> 6; matrix products, arithmetic and copies ran while one was open for 12% -> 17% of each run, Pallas kernels for 0% -> 0%
where the time goes in v1:
time: 624 us; the launch traced here: 615 us
  waiting for transfers between devices  307 us (49%)
  blocking collectives  100 us (16%)
  local copies, waits for them, and re-layouts  71.7 us (11%)
  matrix products  51.9 us (8%)
  other arithmetic  36.4 us (6%)
  starting transfers between devices  32.4 us (5%)
  between operations  14.8 us (2%)
    all_to_all x4, waiting for transfers between devices, route_rows(): lax.all_to_all(rows.reshape(n_ep, -1, rows.shape[-1]), 'ep', split_axis=0...  191 us
    all_gather x1, waiting for transfers between devices, per_device(): lax.all_gather(w_down, 'ctx', axis=1, tiled=True)  58.3 us
    reduce_scatter x1, waiting for transfers between devices, per_device(): lax.psum_scatter(jnp.stack([gate_term, up_term, down_term], axis=1).resha...  57.2 us
    all_gather x1, blocking collectives, per_device(): lax.all_gather(keys[0], 'ctx', axis=0, tiled=True)  46.4 us
    all_gather x1, blocking collectives, per_device(): lax.all_gather(values[0], 'ctx', axis=0, tiled=True)  34.8 us
    all_to_all x4, starting transfers between devices, route_rows(): lax.all_to_all(rows.reshape(n_ep, -1, rows.shape[-1]), 'ep', split_axis=0...  24.2 us
    all_gather x1, blocking collectives, per_device(): lax.all_gather(docs[0], 'ctx', axis=0, tiled=True)  19 us
  transfers between devices with their start and end apart: 9, of which 6 were waited for; matrix products, arithmetic and copies ran while one was open for 17% of the time, Pallas kernels for 0%

profile of v1, /device:TPU:32, one launch (start us, length us, event | category | flops | bytes accessed | tf_op | source)
XLA Modules:
  0.0 614.9 jit_solution(14107199160909766770)
XLA Ops:
  7.2 2.3 stack.27
  9.5 7.1 %all-to-all-start.1 = ((bf16[8,1,256,384]{3,2,1,0:T(8,128)(2,1)}), bf16[8,1,256,384]{3,2,1,0:T(8,128)(2,1)}, u32[]{:S(2)}, u32[]{:S(2)}) async-start(bf16[8,1,256,384]{3,2,1,0:T(8,128)(2,1)} %stack.27), calls=%async_computation.1 | async-start | bytes 3145728 | tf_op jit(solution)/shard_map/all_to_all | solution.py:90
  17.0 46.4 %all-gather = bf16[1,1024,256]{1,2,0:T(8,128)(2,1)S(1)} all-gather(bf16[1,128,256]{1,2,0:T(8,128)(2,1)S(1)} %copy.75), channel_id=2, replica_groups=mesh['ctx'=8,'ep'=32] {'ctx'}, dimensions={1}, use_global_device_ids=true | all-gather | bytes 589824 | tf_op jit(solution)/shard_map/all_gather | solution.py:53
  63.7 19.0 %all-gather.1 = s32[1,1024]{1,0:T(1,128)S(1)} all-gather(s32[1,128]{1,0:T(1,128)S(1)} %copy-done.34), channel_id=3, replica_groups=mesh['ctx'=8,'ep'=32] {'ctx'}, dimensions={1}, use_global_device_ids=true | all-gather | bytes 4608 | tf_op jit(solution)/shard_map/all_gather | solution.py:55
  82.8 34.8 %all-gather.2 = bf16[1,1024,256]{2,1,0:T(8,128)(2,1)S(1)} all-gather(bf16[1,128,256]{2,1,0:T(8,128)(2,1)S(1)} %copy-done.30), channel_id=4, replica_groups=mesh['ctx'=8,'ep'=32] {'ctx'}, dimensions={1}, use_global_device_ids=true | all-gather | bytes 589824 | tf_op jit(solution)/shard_map/all_gather | solution.py:54
  118.0 4.8 fusion.66
  122.8 4.4 fusion.6
  127.2 2.0 bitcast_convert_fusion.3
  132.0 2.1 reshape.437
  135.9 5.4 scatter_custom_fusion
  141.3 2.4 reshape.397
  143.8 9.0 %all-to-all-start = ((bf16[32,20,2048]{2,1,0:T(8,128)(2,1)}), bf16[32,20,2048]{2,1,0:T(8,128)(2,1)}, u32[]{:S(2)}, u32[]{:S(2)}) async-start(bf16[32,20,2048]{2,1,0:T(8,128)(2,1)} %reshape.397), calls=%async_computation | async-start | bytes 6291456 | tf_op jit(solution)/shard_map/all_to_all | solution.py:32
  153.6 3.1 broadcast_in_dim.19
  156.7 5.3 convert_element_type.232
  162.3 6.1 scatter_custom_fusion.1
  168.4 2.4 reshape.403
  170.8 55.0 %all-to-all-done = bf16[32,20,2048]{2,1,0:T(8,128)(2,1)} async-done(((bf16[32,20,2048]{2,1,0:T(8,128)(2,1)}), bf16[32,20,2048]{2,1,0:T(8,128)(2,1)}, u32[]{:S(2)}, u32[]{:S(2)}) %all-to-all-start) | async-done | bytes 2621472 | tf_op jit(solution)/shard_map/all_to_all | solution.py:32
  225.8 4.6 all-to-all-start.3
  231.2 5.2 fusion.21
  236.4 5.2 fusion.67
  241.6 58.3 %all-gather.8.cloned.1.call-done = bf16[1,2048,384]{2,1,0:T(8,128)(2,1)} async-done(((bf16[1,256,384]{2,1,0:T(8,128)(2,1)}), bf16[1,2048,384]{2,1,0:T(8,128)(2,1)}) %all-gather.8.cloned.1.call-update) | async-done | bytes 1572880 | tf_op jit(solution)/shard_map/all_gather | solution.py:99
  299.9 3.4 all-to-all-done.3
  303.3 4.2 fusion.17
  307.6 2.7 fusion.56
  310.3 3.2 fusion.58
  315.0 3.3 copy.93
  318.3 5.5 all-to-all-start.4
  326.5 5.2 fusion.8
  331.7 65.2 %all-to-all-done.4 = bf16[32,20,2048]{2,1,0:T(8,128)(2,1)} async-done(((bf16[32,20,2048]{2,1,0:T(8,128)(2,1)}), bf16[32,20,2048]{2,1,0:T(8,128)(2,1)}, u32[]{:S(2)}, u32[]{:S(2)}) %all-to-all-start.4) | async-done | bytes 2621472 | tf_op jit(solution)/shard_map/all_to_all | solution.py:32
  396.9 3.6 reshape.406
  400.5 3.3 gather_fusion.1
  403.8 4.8 reshape.415
  408.6 4.9 reduce_sum.77
  415.5 2.7 fusion.40
  419.9 4.9 fusion.2
  428.3 4.1 fusion.9
  432.4 4.2 fusion.10
  436.6 2.5 pad_maximum_fusion
  442.1 3.1 copy.89
  445.2 5.1 all-to-all-start.2
  451.7 2.9 fusion.29
  455.6 67.4 %all-to-all-done.2 = bf16[32,20,2048]{2,1,0:T(8,128)(2,1)} async-done(((bf16[32,20,2048]{2,1,0:T(8,128)(2,1)}), bf16[32,20,2048]{2,1,0:T(8,128)(2,1)}, u32[]{:S(2)}, u32[]{:S(2)}) %all-to-all-start.2) | async-done | bytes 2621472 | tf_op jit(solution)/shard_map/all_to_all | solution.py:32
  523.1 3.7 reshape.402
  526.8 3.3 gather_fusion
  530.1 4.9 reshape.412
  535.0 2.7 multiply_reduce_fusion
  538.5 5.7 multiply_reduce_fusion.1
  547.2 57.2 %reduce-scatter.5.cloned.1.call-done = bf16[256,1152]{0,1:T(8,128)(2,1)} async-done(((bf16[2048,1152]{0,1:T(8,128)(2,1)}), bf16[256,1152]{0,1:T(8,128)(2,1)}) %reduce-scatter.5.cloned.1.call-update) | async-done | bytes 589840 | tf_op jit(solution)/shard_map/reduce_scatter | solution.py:122
  (133 shorter events, 31.5 us)
Async XLA Ops:
  7.2 9.4 %copy-start.33 = (s32[1,128,4]{1,2,0:T(4,128)S(1)}, s32[1,128,4]{1,2,0:T(4,128)}, u32[]{:S(2)}) copy-start(s32[1,128,4]{1,2,0:T(4,128)} %param.18) | copy-start | bytes 6148
  7.2 9.7 %copy-start.31 = (bf16[1,128,256]{2,1,0:T(8,128)(2,1)S(1)}, bf16[1,128,256]{2,1,0:T(8,128)(2,1)}, u32[]{:S(2)}) copy-start(bf16[1,128,256]{2,1,0:T(8,128)(2,1)} %param.13) | copy-start | bytes 196612
  7.2 56.2 %copy-start.27 = (bf16[1,128,2048]{2,1,0:T(8,128)(2,1)S(1)}, bf16[1,128,2048]{2,1,0:T(8,128)(2,1)}, u32[]{:S(2)}) copy-start(bf16[1,128,2048]{2,1,0:T(8,128)(2,1)} %param.12) | copy-start | bytes 1572868
  9.5 54.3 %copy-start.34 = (s32[1,128]{1,0:T(1,128)S(1)}, s32[1,128]{1,0:T(1,128)}, u32[]{:S(2)}) copy-start(s32[1,128]{1,0:T(1,128)} %param.15) | copy-start | bytes 1540
  9.5 73.3 %copy-start.30 = (bf16[1,128,256]{2,1,0:T(8,128)(2,1)S(1)}, bf16[1,128,256]{2,1,0:T(8,128)(2,1)}, u32[]{:S(2)}) copy-start(bf16[1,128,256]{2,1,0:T(8,128)(2,1)} %param.14) | copy-start | bytes 196612
  9.5 134.3 %all-to-all-start.1 = ((bf16[8,1,256,384]{3,2,1,0:T(8,128)(2,1)}), bf16[8,1,256,384]{3,2,1,0:T(8,128)(2,1)}, u32[]{:S(2)}, u32[]{:S(2)}) async-start(bf16[8,1,256,384]{3,2,1,0:T(8,128)(2,1)} %stack.27), calls=%async_computation.1 | async-start | bytes 3145728 | tf_op jit(solution)/shard_map/all_to_all | solution.py:90
  63.4 59.3 %copy-start.16 = (bf16[1,1024,256]{1,2,0:T(8,128)(2,1)}, bf16[1,1024,256]{1,2,0:T(8,128)(2,1)S(1)}, u32[]{:S(2)}) copy-start(bf16[1,1024,256]{1,2,0:T(8,128)(2,1)S(1)} %all-gather) | copy-start | bytes 1572868
  63.7 59.1 %copy-start.18 = (bf16[1,128,2048]{1,2,0:T(8,128)(2,1)}, bf16[1,128,2048]{1,2,0:T(8,128)(2,1)S(1)}, u32[]{:S(2)}) copy-start(bf16[1,128,2048]{1,2,0:T(8,128)(2,1)S(1)} %copy.142) | copy-start | bytes 1572868
  117.8 9.4 %copy-start.20 = (bf16[1,1024,256]{1,2,0:T(8,128)(2,1)}, bf16[1,1024,256]{1,2,0:T(8,128)(2,1)S(1)}, u32[]{:S(2)}) copy-start(bf16[1,1024,256]{1,2,0:T(8,128)(2,1)S(1)} %copy.78) | copy-start | bytes 1572868
  127.2 2.1 copy-start
  127.2 2.4 copy-start.9
  129.3 1.6 copy-start.6
  129.3 1.4 copy-start.29
  129.9 0.8 copy-start.12
  143.8 9.7 %copy-start.8 = (bf16[1,128,2048]{2,1,0:T(8,128)(2,1)S(1)}, bf16[1,128,2048]{2,1,0:T(8,128)(2,1)}, u32[]{:S(2)}) copy-start(bf16[1,128,2048]{2,1,0:T(8,128)(2,1)} %param.23) | copy-start | bytes 1572868
  143.8 82.0 %all-to-all-start = ((bf16[32,20,2048]{2,1,0:T(8,128)(2,1)}), bf16[32,20,2048]{2,1,0:T(8,128)(2,1)}, u32[]{:S(2)}, u32[]{:S(2)}) async-start(bf16[32,20,2048]{2,1,0:T(8,128)(2,1)} %reshape.397), calls=%async_computation | async-start | bytes 6291456 | tf_op jit(solution)/shard_map/all_to_all | solution.py:32
  152.8 78.4 %all-gather.6.cloned.1.call-start = ((), (), s32[]{:S(2)}) async-start(), calls=%async_computation.7 | async-start | bytes 1769472 | tf_op jit(solution)/shard_map/all_gather | solution.py:98
  156.7 5.3 copy-start.32
  225.8 77.5 %all-to-all-start.3 = ((bf16[32,20,2048]{2,1,0:T(8,128)(2,1)}), bf16[32,20,2048]{2,1,0:T(8,128)(2,1)}, u32[]{:S(2)}, u32[]{:S(2)}) async-start(bf16[32,20,2048]{2,1,0:T(8,128)(2,1)} %reshape.403), calls=%async_computation.3 | async-start | bytes 6291456 | tf_op jit(solution)/shard_map/all_to_all | solution.py:32
  230.4 69.5 %all-gather.8.cloned.1.call-start = ((), (), s32[]{:S(2)}) async-start(), calls=%async_computation.8 | async-start | bytes 1769472 | tf_op jit(solution)/shard_map/all_gather | solution.py:99
  303.3 4.3 copy-start.26
  310.3 3.2 copy-start.22
  310.3 3.2 copy-start.25
  318.3 7.0 %copy-start.10 = (bf16[1,128,2048]{2,1,0:T(8,128)(2,1)S(1)}, bf16[1,128,2048]{2,1,0:T(8,128)(2,1)}, u32[]{:S(2)}) copy-start(bf16[1,128,2048]{2,1,0:T(8,128)(2,1)} %param.16) | copy-start | bytes 1572868
  318.3 78.6 %all-to-all-start.4 = ((bf16[32,20,2048]{2,1,0:T(8,128)(2,1)}), bf16[32,20,2048]{2,1,0:T(8,128)(2,1)}, u32[]{:S(2)}, u32[]{:S(2)}) async-start(bf16[32,20,2048]{2,1,0:T(8,128)(2,1)} %copy.93), calls=%async_computation.4 | async-start | bytes 6291456 | tf_op jit(solution)/shard_map/all_to_all | solution.py:32
  323.8 221.8 %reduce-scatter.3.cloned.1.call-start = ((), (), s32[]{:S(2)}) async-start(), calls=%async_computation.9 | async-start | bytes 1179648 | tf_op jit(solution)/shard_map/reduce_scatter | solution.py:174
  408.6 6.2 %copy-start.13 = (bf16[128,2048]{1,0:T(8,128)(2,1)S(1)}, bf16[128,2048]{1,0:T(8,128)(2,1)}, u32[]{:S(2)}) copy-start(bf16[128,2048]{1,0:T(8,128)(2,1)} %copy-done.12) | copy-start | bytes 1572868
  413.5 4.7 copy-start.4
  413.5 2.0 copy-start.14
  414.8 3.3 copy-start.1
  418.2 1.7 copy-start.21
  419.9 4.9 copy-start.19
  424.8 1.9 copy-start.3
  426.8 1.6 copy-start.23
  428.1 4.3 copy-start.28
  428.1 176.3 %reduce-scatter.5.cloned.1.call-start = ((), (), s32[]{:S(2)}) async-start(), calls=%async_computation.10 | async-start | bytes 5308416 | tf_op jit(solution)/shard_map/reduce_scatter | solution.py:122
  432.4 4.2 copy-start.24
  439.1 1.4 copy-start.35
  445.2 5.2 copy-start.7
  445.2 6.5 %copy-start.17 = (bf16[1,1024,256]{1,2,0:T(8,128)(2,1)S(1)}, bf16[1,1024,256]{1,2,0:T(8,128)(2,1)}, u32[]{:S(2)}) copy-start(bf16[1,1024,256]{1,2,0:T(8,128)(2,1)} %copy-done.16) | copy-start | bytes 1572868
  445.2 77.9 %all-to-all-start.2 = ((bf16[32,20,2048]{2,1,0:T(8,128)(2,1)}), bf16[32,20,2048]{2,1,0:T(8,128)(2,1)}, u32[]{:S(2)}, u32[]{:S(2)}) async-start(bf16[32,20,2048]{2,1,0:T(8,128)(2,1)} %copy.89), calls=%async_computation.2 | async-start | bytes 6291456 | tf_op jit(solution)/shard_map/all_to_all | solution.py:32
  530.1 4.9 copy-start.2
  538.5 5.7 copy-start.5
  538.5 5.7 copy-start.11
  538.5 5.7 copy-start.15
Sparse Core Ops, SparseCore 0:
  156.1 66.1 all-gather.5
  233.8 66.0 all-gather.7
  428.2 76.5 reduce-scatter.2
  508.8 95.4 reduce-scatter.4
